TPU v7x, 32 devices: a whole 2x2x4 slice. The times are simulated.
32 devices in a mesh: section: 2 (over core), ctx: 8 (over z, x), tp: 2 (over y).
Axes of the slice: x: 2, y: 2, z: 4, core: 2. Of those that a mesh axis runs over, the one named last changes fastest.
Arguments:
- layer_input: bfloat16 [2, 1024, 1024], P(None, 'ctx'), may hold values from -6 to 6
- cotangent: bfloat16 [2, 1024, 1024], P(None, 'ctx'), may hold values from -6 to 6
- w_qkv: bfloat16 [2, 1024, 3, 1024], P('section', None, None, 'tp'), may hold values from -0.1875 to 0.1875
- b_qv: bfloat16 [2, 2, 1024], P('section', None, 'tp'), may hold values from -3 to 3
- w_out: bfloat16 [2, 1024, 1024], P('section', 'tp'), may hold values from -4 to 4
- b_out: bfloat16 [2, 1024], P('section'), may hold values from -3 to 3
- w_fc: bfloat16 [2, 1024, 4096], P('section', None, 'tp'), may hold values from -0.1875 to 0.1875
- b_fc: bfloat16 [2, 4096], P('section', 'tp'), may hold values from -3 to 3
- w_proj: bfloat16 [2, 4096, 1024], P('section', 'tp'), may hold values from -0.09375 to 0.09375
- b_proj: bfloat16 [2, 1024], P('section'), may hold values from -3 to 3
- ln_gain: float32 [2, 2, 1024], P('section'), may hold values from 0.5 to 1.5
- ln_bias: float32 [2, 2, 1024], P('section'), may hold values from -3 to 3
Outputs:
- activations: bfloat16 [2, 2, 1024, 1024], P('section', None, 'ctx')
- input_grads: float32 [2, 2, 1024, 1024], P('section', None, 'ctx')
- grad_w_qkv: float32 [2, 1024, 3, 1024], P('section', None, None, 'tp')
- grad_b_qv: float32 [2, 2, 1024], P('section', None, 'tp')
- grad_w_out: float32 [2, 1024, 1024], P('section', 'tp')
- grad_b_out: float32 [2, 1024], P('section')
- grad_w_fc: float32 [2, 1024, 4096], P('section', None, 'tp')
- grad_b_fc: float32 [2, 4096], P('section', 'tp')
- grad_w_proj: float32 [2, 4096, 1024], P('section', 'tp')
- grad_b_proj: float32 [2, 1024], P('section')
- grad_ln_gain: float32 [2, 2, 1024], P('section')
- grad_ln_bias: float32 [2, 2, 1024], P('section')
All inputs are finite; a program needn't handle non-finite values.
Results may differ from a plain program's by a relative error of at most 0.028.
Values may be sent and summed in bfloat16 or wider, within the bound.
A program may use at most 192 MiB of HBM per device.

v0:
```python
import jax
import jax.numpy as jnp
from jax import lax
from jax.sharding import PartitionSpec as P

HD = 64
EPS = 1e-05
GELU_C = 0.7978845608028654


def shifted(value, axis, steps):
    count = lax.axis_size(axis)
    first, last = (max(0, -steps), min(count, count - steps))
    return lax.ppermute(value, axis, [(source, source + steps) for source in range(first, last)])


def norm_forward(values, gain_vec, shift_vec):
    row_mean = jnp.mean(values, axis=-1, keepdims=True)
    centered = values - row_mean
    inv_std = lax.rsqrt(jnp.mean(centered * centered, axis=-1, keepdims=True) + EPS)
    normed = centered * inv_std
    return (normed * gain_vec + shift_vec, normed, inv_std)


def norm_backward(upstream, normed, inv_std, gain_vec):
    dnormed = upstream * gain_vec
    centered_grad = (
        dnormed
        - jnp.mean(dnormed, axis=-1, keepdims=True)
        - normed * jnp.mean(dnormed * normed, axis=-1, keepdims=True)
    )
    return (inv_std * centered_grad, jnp.sum(upstream * normed, axis=0), jnp.sum(upstream, axis=0))


def gelu_parts(pre_act):
    tanh_val = jnp.tanh(GELU_C * (pre_act + 0.044715 * pre_act * pre_act * pre_act))
    gelu_value = 0.5 * pre_act * (1.0 + tanh_val)
    gelu_slope = 0.5 * (1.0 + tanh_val) + 0.5 * pre_act * (1.0 - tanh_val * tanh_val) * GELU_C * (
        1.0 + 3.0 * 0.044715 * pre_act * pre_act
    )
    return (gelu_value, gelu_slope)


def split_heads(values, head_count):
    return values.reshape(values.shape[0], head_count, values.shape[1] // head_count)


def fold_keys(running, block_kv, queries, query_pos, head_count):
    totals, accum = running
    key_rows, val_rows = block_kv
    head_q = split_heads(queries, head_count)
    head_k = split_heads(key_rows, head_count)
    head_v = split_heads(val_rows, head_count)
    score_scale = HD ** (-0.5)
    scores = (
        jnp.einsum("qhd,khd->hqk", head_q, head_k, preferred_element_type=jnp.float32) * score_scale
    )
    key_pos = jnp.arange(key_rows.shape[0], dtype=jnp.int32)
    causal = query_pos[:, None] >= key_pos[None, :]
    weights = jnp.where(causal[None], jnp.exp(scores), 0.0)
    totals = jnp.sum(weights, axis=-1).T
    portion = jnp.einsum(
        "hqk,khd->qhd", weights.astype(jnp.bfloat16), head_v, preferred_element_type=jnp.float32
    )
    return (totals, portion.reshape(accum.shape))


def layer_forward(layer_in, weights_set, query_pos):
    w_qkv, b_qv, w_out, b_out, w_fc, b_fc, w_proj, b_proj, ln_gain, ln_bias = weights_set
    row_count, model_width = layer_in.shape
    local_cols = w_qkv.shape[2]
    head_count = local_cols // HD
    layer_f32 = layer_in.astype(jnp.float32)
    first_norm, normed_a, inv_a = norm_forward(layer_f32, ln_gain[0], ln_bias[0])
    first_bf = first_norm.astype(jnp.bfloat16)
    joined = jnp.dot(
        first_bf, w_qkv.reshape(model_width, 3 * local_cols), preferred_element_type=jnp.float32
    )
    queries = (joined[:, :local_cols] + b_qv[0].astype(jnp.float32)).astype(jnp.bfloat16)
    key_rows = joined[:, local_cols : 2 * local_cols].astype(jnp.bfloat16)
    val_rows = (joined[:, 2 * local_cols :] + b_qv[1].astype(jnp.float32)).astype(jnp.bfloat16)
    init_state = (
        jnp.zeros((row_count, head_count), jnp.float32),
        jnp.zeros((row_count, local_cols), jnp.float32),
    )
    totals, accum = fold_keys(
        init_state,
        (
            lax.all_gather(key_rows, "ctx", axis=0, tiled=True),
            lax.all_gather(val_rows, "ctx", axis=0, tiled=True),
        ),
        queries,
        query_pos,
        head_count,
    )
    held_keys = (key_rows, val_rows)
    attended = (
        (accum.reshape(row_count, head_count, HD) / totals[:, :, None])
        .reshape(row_count, local_cols)
        .astype(jnp.bfloat16)
    )
    log_total = jnp.log(totals)
    attn_mixed = lax.psum(
        jnp.dot(attended, w_out, preferred_element_type=jnp.float32).astype(jnp.bfloat16), "tp"
    ).astype(jnp.float32)
    hidden_in = layer_f32 + attn_mixed + b_out.astype(jnp.float32)
    second_norm, normed_b, inv_b = norm_forward(hidden_in, ln_gain[1], ln_bias[1])
    second_bf = second_norm.astype(jnp.bfloat16)
    pre_act = jnp.dot(second_bf, w_fc, preferred_element_type=jnp.float32) + b_fc.astype(
        jnp.float32
    )
    gelu_value, gelu_slope = gelu_parts(pre_act)
    act_bf = gelu_value.astype(jnp.bfloat16)
    mlp_mixed = lax.psum(
        jnp.dot(act_bf, w_proj, preferred_element_type=jnp.float32).astype(jnp.bfloat16), "tp"
    ).astype(jnp.float32)
    result = hidden_in + mlp_mixed + b_proj.astype(jnp.float32)
    saved = (
        normed_a,
        inv_a,
        first_bf,
        queries,
        (key_rows, val_rows),
        held_keys,
        attended,
        log_total,
        normed_b,
        inv_b,
        second_bf,
        act_bf,
        gelu_slope,
    )
    return (result.astype(jnp.bfloat16), saved)


def layer_backward(upstream, saved, weights_set, query_pos):
    w_qkv, b_qv, w_out, b_out, w_fc, b_fc, w_proj, b_proj, ln_gain, ln_bias = weights_set
    (
        normed_a,
        inv_a,
        first_bf,
        queries,
        own_kv,
        held_keys,
        attended,
        log_total,
        normed_b,
        inv_b,
        second_bf,
        act_bf,
        gelu_slope,
    ) = saved
    row_count, model_width = upstream.shape
    local_cols = w_qkv.shape[2]
    head_count = local_cols // HD
    score_scale = HD ** (-0.5)
    up_bf = upstream.astype(jnp.bfloat16)
    grad_b_proj = jnp.sum(upstream, axis=0)
    grad_w_proj = jnp.dot(act_bf.T, up_bf, preferred_element_type=jnp.float32)
    d_pre = jnp.dot(up_bf, w_proj.T, preferred_element_type=jnp.float32) * gelu_slope
    d_pre_bf = d_pre.astype(jnp.bfloat16)
    grad_b_fc = jnp.sum(d_pre, axis=0)
    grad_w_fc = jnp.dot(second_bf.T, d_pre_bf, preferred_element_type=jnp.float32)
    d_second = lax.psum(
        jnp.dot(d_pre_bf, w_fc.T, preferred_element_type=jnp.float32).astype(jnp.bfloat16), "tp"
    ).astype(jnp.float32)
    d_hidden_ln, gain_b, shift_b = norm_backward(d_second, normed_b, inv_b, ln_gain[1])
    d_hidden = upstream + d_hidden_ln
    grad_b_out = jnp.sum(d_hidden, axis=0)
    hidden_bf = d_hidden.astype(jnp.bfloat16)
    grad_w_out = jnp.dot(attended.T, hidden_bf, preferred_element_type=jnp.float32)
    d_attended = jnp.dot(hidden_bf, w_out.T, preferred_element_type=jnp.float32).astype(
        jnp.bfloat16
    )
    all_keys, all_vals = (
        lax.all_gather(held_keys[0], "ctx", axis=0, tiled=True),
        lax.all_gather(held_keys[1], "ctx", axis=0, tiled=True),
    )
    head_q = split_heads(queries, head_count)
    head_k = split_heads(all_keys, head_count)
    head_v = split_heads(all_vals, head_count)
    head_d = split_heads(d_attended, head_count)
    scores = (
        jnp.einsum("qhd,khd->hqk", head_q, head_k, preferred_element_type=jnp.float32) * score_scale
    )
    key_pos = jnp.arange(all_keys.shape[0], dtype=jnp.int32)
    causal = query_pos[:, None] >= key_pos[None, :]
    probs = jnp.where(causal[None], jnp.exp(scores - log_total.T[:, :, None]), 0.0)
    row_delta = jnp.sum(
        d_attended.astype(jnp.float32).reshape(row_count, head_count, HD)
        * attended.astype(jnp.float32).reshape(row_count, head_count, HD),
        axis=-1,
    )
    d_probs = jnp.einsum("qhd,khd->hqk", head_d, head_v, preferred_element_type=jnp.float32)
    d_scores = (probs * (d_probs - row_delta.T[:, :, None])).astype(jnp.bfloat16)
    d_query = (
        jnp.einsum("hqk,khd->qhd", d_scores, head_k, preferred_element_type=jnp.float32).reshape(
            row_count, local_cols
        )
        * score_scale
    )
    key_term = (
        jnp.einsum("hqk,qhd->khd", d_scores, head_q, preferred_element_type=jnp.float32).reshape(
            all_keys.shape[0], local_cols
        )
        * score_scale
    )
    val_term = jnp.einsum(
        "hqk,qhd->khd", probs.astype(jnp.bfloat16), head_d, preferred_element_type=jnp.float32
    ).reshape(all_keys.shape[0], local_cols)
    d_key, d_val = (
        lax.psum_scatter(
            key_term.astype(jnp.bfloat16), "ctx", scatter_dimension=0, tiled=True
        ).astype(jnp.float32),
        lax.psum_scatter(
            val_term.astype(jnp.bfloat16), "ctx", scatter_dimension=0, tiled=True
        ).astype(jnp.float32),
    )
    grad_b_qv = jnp.stack([jnp.sum(d_query, axis=0), jnp.sum(d_val, axis=0)])
    d_joined = jnp.concatenate([d_query, d_key, d_val], axis=1).astype(jnp.bfloat16)
    grad_w_qkv = jnp.dot(first_bf.T, d_joined, preferred_element_type=jnp.float32).reshape(
        model_width, 3, local_cols
    )
    d_first = lax.psum(
        jnp.dot(
            d_joined,
            w_qkv.reshape(model_width, 3 * local_cols).T,
            preferred_element_type=jnp.float32,
        ).astype(jnp.bfloat16),
        "tp",
    ).astype(jnp.float32)
    d_in_ln, gain_a, shift_a = norm_backward(d_first, normed_a, inv_a, ln_gain[0])
    d_input = d_hidden + d_in_ln
    grads = (
        grad_w_qkv,
        grad_b_qv,
        grad_w_out,
        grad_b_out,
        grad_w_fc,
        grad_b_fc,
        grad_w_proj,
        grad_b_proj,
        jnp.stack([gain_a, gain_b]),
        jnp.stack([shift_a, shift_b]),
    )
    return (d_input, grads)


def body(
    layer_input, cotangent, w_qkv, b_qv, w_out, b_out, w_fc, b_fc, w_proj, b_proj, ln_gain, ln_bias
):
    weights_set = (
        w_qkv[0],
        b_qv[0],
        w_out[0],
        b_out[0],
        w_fc[0],
        b_fc[0],
        w_proj[0],
        b_proj[0],
        ln_gain[0],
        ln_bias[0],
    )
    later_segment = lax.axis_index("section") == 1
    micro, row_count, model_width = layer_input.shape
    query_pos = lax.axis_index("ctx") * row_count + jnp.arange(row_count, dtype=jnp.int32)
    incoming = jnp.zeros((row_count, model_width), jnp.bfloat16)
    results = []
    saved_ticks = []
    for tick_index in range(micro + 1):
        if tick_index < micro:
            fresh_input = layer_input[tick_index]
        else:
            fresh_input = jnp.zeros((row_count, model_width), jnp.bfloat16)
        layer_in = jnp.where(later_segment, incoming, fresh_input)
        result, saved = layer_forward(layer_in, weights_set, query_pos)
        results.append(result)
        saved_ticks.append(saved)
        if tick_index < micro:
            incoming = shifted(result, "section", 1)
    outgoing = jnp.zeros((row_count, model_width), jnp.float32)
    grad_totals = []
    input_grads_all = []
    for tick_index in range(micro + 1):
        if tick_index < micro:
            given_grad = cotangent[tick_index].astype(jnp.float32)
        else:
            given_grad = jnp.zeros((row_count, model_width), jnp.float32)
        upstream = jnp.where(later_segment, given_grad, outgoing)
        saved = jax.tree.map(
            lambda late_val, early_val: jnp.where(later_segment, late_val, early_val),
            saved_ticks[min(tick_index + 1, micro)],
            saved_ticks[max(tick_index - 1, 0)],
        )
        d_input, grads = layer_backward(upstream, saved, weights_set, query_pos)
        if tick_index == 0:
            grad_totals = grads
        else:
            grad_totals = jax.tree.map(jnp.add, grad_totals, grads)
        input_grads_all.append(d_input)
        if tick_index < micro:
            outgoing = shifted(d_input.astype(jnp.bfloat16), "section", -1).astype(d_input.dtype)
    activations = jnp.stack(
        [
            jnp.where(later_segment, results[batch_index + 1], results[batch_index])
            for batch_index in range(micro)
        ]
    )[None]
    input_grads = jnp.stack(
        [
            jnp.where(later_segment, input_grads_all[batch_index], input_grads_all[batch_index + 1])
            for batch_index in range(micro)
        ]
    )[None]
    summed = (
        lax.psum(grad_totals[0].astype(jnp.bfloat16), "ctx").astype(jnp.float32),
        lax.psum(grad_totals[1].astype(jnp.bfloat16), "ctx").astype(jnp.float32),
        lax.psum(grad_totals[2].astype(jnp.bfloat16), "ctx").astype(jnp.float32),
        lax.psum(grad_totals[3].astype(jnp.bfloat16), "ctx").astype(jnp.float32),
        lax.psum(grad_totals[4].astype(jnp.bfloat16), "ctx").astype(jnp.float32),
        lax.psum(grad_totals[5].astype(jnp.bfloat16), "ctx").astype(jnp.float32),
        lax.psum(grad_totals[6].astype(jnp.bfloat16), "ctx").astype(jnp.float32),
        lax.psum(grad_totals[7].astype(jnp.bfloat16), "ctx").astype(jnp.float32),
        lax.psum(grad_totals[8].astype(jnp.bfloat16), "ctx").astype(jnp.float32),
        lax.psum(grad_totals[9].astype(jnp.bfloat16), "ctx").astype(jnp.float32),
    )
    return (
        activations,
        input_grads,
        summed[0][None],
        summed[1][None],
        summed[2][None],
        summed[3][None],
        summed[4][None],
        summed[5][None],
        summed[6][None],
        summed[7][None],
        summed[8][None],
        summed[9][None],
    )


def solution(mesh):
    placed = (
        P(None, "ctx", None),
        P(None, "ctx", None),
        P("section", None, None, "tp"),
        P("section", None, "tp"),
        P("section", "tp", None),
        P("section", None),
        P("section", None, "tp"),
        P("section", "tp"),
        P("section", "tp", None),
        P("section", None),
        P("section", None, None),
        P("section", None, None),
    )
    return jax.shard_map(
        body,
        mesh=mesh,
        in_specs=placed,
        out_specs=(
            P("section", None, "ctx", None),
            P("section", None, "ctx", None),
            P("section", None, None, "tp"),
            P("section", None, "tp"),
            P("section", "tp", None),
            P("section", None),
            P("section", None, "tp"),
            P("section", "tp"),
            P("section", "tp", None),
            P("section", None),
            P("section", None, None),
            P("section", None, None),
        ),
        check_vma=False,
    )
```

profile of v0, /device:TPU:0, one launch (start us, length us, event | category | flops | bytes accessed | tf_op | source)
XLA Modules:
  0.0 1655.5 jit_solution(18073447266085569030)
XLA Ops:
  11.3 4.7 copy.76
  21.0 42.0 %all-gather.15.cloned.1.call-done = bf16[1024,512]{1,0:T(8,128)(2,1)} async-done(((bf16[128,512]{1,0:T(8,128)(2,1)}), bf16[1024,512]{1,0:T(8,128)(2,1)}) %all-gather.15.cloned.1.call-update) | async-done | bytes 1048592 | tf_op jit(solution)/shard_map/all_gather | solution.py:89
  65.2 4.4 fusion.24
  69.6 34.5 %all-gather.13.cloned.1.call-done = bf16[1024,512]{1,0:T(8,128)(2,1)} async-done(((bf16[128,512]{1,0:T(8,128)(2,1)}), bf16[1024,512]{1,0:T(8,128)(2,1)}) %all-gather.13.cloned.1.call-update) | async-done | bytes 1048592 | tf_op jit(solution)/shard_map/all_gather | solution.py:90
  105.6 3.1 fusion.138
  109.9 22.1 %all-reduce.16.cloned.1.call-done = bf16[128,1024]{1,0:T(8,128)(2,1)} async-done(((bf16[128,1024]{1,0:T(8,128)(2,1)}), bf16[128,1024]{1,0:T(8,128)(2,1)}) %all-reduce.16.cloned.1.call-update) | async-done | bytes 262160 | tf_op jit(solution)/shard_map/psum | solution.py:103
  134.5 3.1 fusion.35
  139.4 23.4 %all-reduce.18.cloned.1.call-done = bf16[128,1024]{1,0:T(8,128)(2,1)} async-done(((bf16[128,1024]{1,0:T(8,128)(2,1)}), bf16[128,1024]{1,0:T(8,128)(2,1)}) %all-reduce.18.cloned.1.call-update) | async-done | bytes 262160 | tf_op jit(solution)/shard_map/psum | solution.py:114
  173.6 39.7 %all-gather.19.cloned.1.call-done = bf16[1024,512]{1,0:T(8,128)(2,1)} async-done(((bf16[128,512]{1,0:T(8,128)(2,1)}), bf16[1024,512]{1,0:T(8,128)(2,1)}) %all-gather.19.cloned.1.call-update) | async-done | bytes 1048592 | tf_op jit(solution)/shard_map/all_gather | solution.py:89
  215.6 5.0 fusion.26
  220.6 33.7 %all-gather.17.cloned.1.call-done = bf16[1024,512]{1,0:T(8,128)(2,1)} async-done(((bf16[128,512]{1,0:T(8,128)(2,1)}), bf16[1024,512]{1,0:T(8,128)(2,1)}) %all-gather.17.cloned.1.call-update) | async-done | bytes 1048592 | tf_op jit(solution)/shard_map/all_gather | solution.py:90
  256.6 3.4 fusion.132
  261.6 21.6 %all-reduce.20.cloned.1.call-done = bf16[128,1024]{1,0:T(8,128)(2,1)} async-done(((bf16[128,1024]{1,0:T(8,128)(2,1)}), bf16[128,1024]{1,0:T(8,128)(2,1)}) %all-reduce.20.cloned.1.call-update) | async-done | bytes 262160 | tf_op jit(solution)/shard_map/psum | solution.py:103
  286.2 3.1 fusion.38
  297.9 28.0 %all-reduce.34.cloned.1.call-done = (bf16[128,1024]{1,0:T(8,128)(2,1)}, bf16[128,1024]{1,0:T(8,128)(2,1)}) async-done(((bf16[128,1024]{1,0:T(8,128)(2,1)}, bf16[128,1024]{1,0:T(8,128)(2,1)}), (bf16[128,1024]{1,0:T(8,128)(2,1)}, bf16[128,1024]{1,0:T(8,128)(2,1)})) %all-reduce.34.cloned.1.call-update) | async-done | bytes 524304 | tf_op jit(solution)/shard_map/psum | solution.py:164
  338.4 30.5 %all-gather.25.cloned.1.call-done = bf16[1024,512]{1,0:T(8,128)(2,1)} async-done(((bf16[128,512]{1,0:T(8,128)(2,1)}), bf16[1024,512]{1,0:T(8,128)(2,1)}) %all-gather.25.cloned.1.call-update) | async-done | bytes 1048592 | tf_op jit(solution)/shard_map/all_gather | solution.py:176
  371.2 4.0 fusion.384
  381.8 28.1 %all-gather.23.cloned.1.call-done = bf16[1024,512]{1,0:T(8,128)(2,1)} async-done(((bf16[128,512]{1,0:T(8,128)(2,1)}), bf16[1024,512]{1,0:T(8,128)(2,1)}) %all-gather.23.cloned.1.call-update) | async-done | bytes 1048592 | tf_op jit(solution)/shard_map/all_gather | solution.py:89
  412.2 4.6 fusion.28
  422.1 28.9 %all-gather.27.cloned.1.call-done = bf16[1024,512]{1,0:T(8,128)(2,1)} async-done(((bf16[128,512]{1,0:T(8,128)(2,1)}), bf16[1024,512]{1,0:T(8,128)(2,1)}) %all-gather.27.cloned.1.call-update) | async-done | bytes 1048592 | tf_op jit(solution)/shard_map/all_gather | solution.py:177
  454.9 4.2 multiply_convert_fusion.2
  464.2 27.8 %all-gather.21.cloned.1.call-done = bf16[1024,512]{1,0:T(8,128)(2,1)} async-done(((bf16[128,512]{1,0:T(8,128)(2,1)}), bf16[1024,512]{1,0:T(8,128)(2,1)}) %all-gather.21.cloned.1.call-update) | async-done | bytes 1048592 | tf_op jit(solution)/shard_map/all_gather | solution.py:90
  494.3 3.5 fusion.126
  500.4 58.6 %reduce-scatter.21.cloned.1.call-done = bf16[128,512]{1,0:T(8,128)(2,1)} async-done(((bf16[1024,512]{1,0:T(8,128)(2,1)}), bf16[128,512]{1,0:T(8,128)(2,1)}) %reduce-scatter.21.cloned.1.call-update) | async-done | bytes 131088
  560.1 65.4 %reduce-scatter.19.cloned.1.call-done = bf16[128,512]{1,0:T(8,128)(2,1)} async-done(((bf16[1024,512]{1,0:T(8,128)(2,1)}), bf16[128,512]{1,0:T(8,128)(2,1)}) %reduce-scatter.19.cloned.1.call-update) | async-done | bytes 131088
  626.5 3.3 convolution_convert_fusion.2
  631.6 26.0 %all-reduce.32.cloned.1.call-done = (bf16[128,1024]{1,0:T(8,128)(2,1)}, bf16[128,1024]{1,0:T(8,128)(2,1)}) async-done(((bf16[128,1024]{1,0:T(8,128)(2,1)}, bf16[128,1024]{1,0:T(8,128)(2,1)}), (bf16[128,1024]{1,0:T(8,128)(2,1)}, bf16[128,1024]{1,0:T(8,128)(2,1)})) %all-reduce.32.cloned.1.call-update) | async-done | bytes 524304 | tf_op jit(solution)/shard_map/psum | solution.py:224
  666.7 3.2 fusion.41
  670.0 3.1 fusion.383
  677.7 22.7 %all-gather.29.cloned.1.call-done = bf16[1024,512]{1,0:T(8,128)(2,1)} async-done(((bf16[128,512]{1,0:T(8,128)(2,1)}), bf16[1024,512]{1,0:T(8,128)(2,1)}) %all-gather.29.cloned.1.call-update) | async-done | bytes 1048592 | tf_op jit(solution)/shard_map/all_gather | solution.py:176
  702.7 4.0 fusion.385
  706.7 18.5 %all-reduce.22.cloned.1.call-done = bf16[128,1024]{1,0:T(8,128)(2,1)} async-done(((bf16[128,1024]{1,0:T(8,128)(2,1)}), bf16[128,1024]{1,0:T(8,128)(2,1)}) %all-reduce.22.cloned.1.call-update) | async-done | bytes 262160 | tf_op jit(solution)/shard_map/psum | solution.py:164
  732.0 4.3 fusion.89
  738.7 28.7 %all-gather.31.cloned.1.call-done = bf16[1024,512]{1,0:T(8,128)(2,1)} async-done(((bf16[128,512]{1,0:T(8,128)(2,1)}), bf16[1024,512]{1,0:T(8,128)(2,1)}) %all-gather.31.cloned.1.call-update) | async-done | bytes 1048592 | tf_op jit(solution)/shard_map/all_gather | solution.py:177
  771.4 4.2 multiply_convert_fusion.1
  780.7 6.1 fusion.275
  786.9 4.9 fusion.245
  795.2 13.4 all-gather.33.cloned.1.call-done
  810.9 38.7 %all-gather.35.cloned.1.call-done = bf16[1024,512]{1,0:T(8,128)(2,1)} async-done(((bf16[128,512]{1,0:T(8,128)(2,1)}), bf16[1024,512]{1,0:T(8,128)(2,1)}) %all-gather.35.cloned.1.call-update) | async-done | bytes 1048592 | tf_op jit(solution)/shard_map/all_gather | solution.py:177
  851.9 4.3 fusion.386
  858.3 57.7 %reduce-scatter.25.cloned.1.call-done = bf16[128,512]{1,0:T(8,128)(2,1)} async-done(((bf16[1024,512]{1,0:T(8,128)(2,1)}), bf16[128,512]{1,0:T(8,128)(2,1)}) %reduce-scatter.25.cloned.1.call-update) | async-done | bytes 131088
  917.6 65.0 %reduce-scatter.23.cloned.1.call-done = bf16[128,512]{1,0:T(8,128)(2,1)} async-done(((bf16[1024,512]{1,0:T(8,128)(2,1)}), bf16[128,512]{1,0:T(8,128)(2,1)}) %reduce-scatter.23.cloned.1.call-update) | async-done | bytes 131088
  984.3 3.4 convolution_convert_fusion.1
  988.2 4.9 fusion.280
  993.1 17.1 %all-reduce.24.cloned.1.call-done = bf16[128,1024]{1,0:T(8,128)(2,1)} async-done(((bf16[128,1024]{1,0:T(8,128)(2,1)}), bf16[128,1024]{1,0:T(8,128)(2,1)}) %all-reduce.24.cloned.1.call-update) | async-done | bytes 262160 | tf_op jit(solution)/shard_map/psum | solution.py:224
  1016.8 3.8 fusion.111
  1026.8 6.6 fusion.243
  1033.3 17.6 %all-reduce.26.cloned.1.call-done = bf16[128,1024]{1,0:T(8,128)(2,1)} async-done(((bf16[128,1024]{1,0:T(8,128)(2,1)}), bf16[128,1024]{1,0:T(8,128)(2,1)}) %all-reduce.26.cloned.1.call-update) | async-done | bytes 262160 | tf_op jit(solution)/shard_map/psum | solution.py:164
  1058.5 4.3 fusion.92
  1065.4 6.1 fusion.273
  1073.3 3.9 fusion.278
  1084.5 9.6 fusion.30
  1094.1 9.2 fusion.31
  1107.2 22.2 %reduce-scatter.29.cloned.1.call-done = bf16[128,512]{1,0:T(8,128)(2,1)} async-done(((bf16[1024,512]{1,0:T(8,128)(2,1)}), bf16[128,512]{1,0:T(8,128)(2,1)}) %reduce-scatter.29.cloned.1.call-update) | async-done | bytes 131088
  1130.5 65.4 %reduce-scatter.27.cloned.1.call-done = bf16[128,512]{1,0:T(8,128)(2,1)} async-done(((bf16[1024,512]{1,0:T(8,128)(2,1)}), bf16[128,512]{1,0:T(8,128)(2,1)}) %reduce-scatter.27.cloned.1.call-update) | async-done | bytes 131088
  1196.9 3.2 convolution_convert_fusion
  1200.3 7.5 add_convert_fusion.2
  1207.8 4.6 copy.98
  1222.7 5.3 all-reduce.30.cloned.1.call-done
  1230.8 39.5 %all-reduce = (bf16[1,2,512]{2,1,0:T(2,128)(2,1)S(1)}, bf16[1,1024]{1,0:T(2,128)(2,1)S(1)}, bf16[1,2048]{1,0:T(2,128)(2,1)S(1)}, bf16[1,1024]{1,0:T(2,128)(2,1)S...) all-reduce(bf16[1,2,512]{2,1,0:T(2,128)(2,1)S(1)} %fusion.327, ...), channel_id=1, replica_groups=mesh['section'=2,'ctx'=8,'tp'=2] {'ctx'}, use_global_device_ids=true, to_apply=%region_55.56 | all-reduce | flops 9216 | bytes 36864 | tf_op jit(solution)/shard_map/psum | solution.py:317
  1279.3 349.7 %all-reduce.28.cloned.1.call-done = (bf16[1,1024,3,512]{1,3,2,0:T(8,128)(2,1)}, bf16[1,512,1024]{2,1,0:T(8,128)(2,1)}, bf16[1,1024,2048]{2,1,0:T(8,128)(2,1)}, bf16[1,2048,1024]{2,1,0:T(8,128)(2,1)}) async-done(((bf16[1,1024,3,512]{1,3,2,0:T(8,128)(2,1)}, bf16[1,512,1024]{2,1,0:T(8,128)(2,1)}, bf16[1,1024,2048]{2,1,0:T(8,128)(2,1)}, bf16[1,2048,1024]{2,1,0:T(8,128)(2,1)}), ...) | async-done | bytes 12582928 | tf_op jit(solution)/shard_map/psum | solution.py:316
  1631.8 5.4 copy.99
  1637.2 6.8 broadcast_in_dim.177
  1644.0 4.4 broadcast_in_dim.181
  (525 shorter events, 202.8 us)
Async XLA Ops:
  7.2 101.5 %copy-start = (bf16[1,512,1024]{2,1,0:T(8,128)(2,1)S(1)}, bf16[1,512,1024]{2,1,0:T(8,128)(2,1)}, u32[]{:S(2)}) copy-start(bf16[1,512,1024]{2,1,0:T(8,128)(2,1)} %param.16) | copy-start | bytes 3145732
  7.2 55.7 %all-gather.15.cloned.1.call-start = ((), (), s32[]{:S(2)}) async-start(), calls=%async_computation.7 | async-start | bytes 1179648 | tf_op jit(solution)/shard_map/all_gather | solution.py:89
  11.2 123.3 %copy-start.80 = (f32[1,1,1024]{2,1,0:T(1,128)}, f32[1,1,1024]{2,1,0:T(1,128)S(1)}, u32[]{:S(2)}) copy-start(f32[1,1,1024]{2,1,0:T(1,128)S(1)} %get-tuple-element.132) | copy-start | bytes 12292
  19.1 50.6 %copy-start.38 = (f32[128,1536]{1,0:T(8,128)}, f32[128,1536]{1,0:T(8,128)S(1)}, u32[]{:S(2)}) copy-start(f32[128,1536]{1,0:T(8,128)S(1)} %fusion.264) | copy-start | bytes 2359300
  19.8 84.3 %all-gather.13.cloned.1.call-start = ((), (), s32[]{:S(2)}) async-start(), calls=%async_computation.6 | async-start | bytes 1179648 | tf_op jit(solution)/shard_map/all_gather | solution.py:90
  19.9 49.7 %copy-start.114 = (f32[1,1,512]{2,1,0:T(1,128)}, f32[1,1,512]{2,1,0:T(1,128)S(1)}, u32[]{:S(2)}) copy-start(f32[1,1,512]{2,1,0:T(1,128)S(1)} %get-tuple-element.136) | copy-start | bytes 6148
  19.9 49.7 %copy-start.115 = (f32[1,1,512]{2,1,0:T(1,128)}, f32[1,1,512]{2,1,0:T(1,128)S(1)}, u32[]{:S(2)}) copy-start(f32[1,1,512]{2,1,0:T(1,128)S(1)} %get-tuple-element.137) | copy-start | bytes 6148
  20.6 150.3 %copy-start.50 = (bf16[128,512]{1,0:T(8,128)(2,1)}, bf16[128,512]{1,0:T(8,128)(2,1)S(1)}, u32[]{:S(2)}) copy-start(bf16[128,512]{1,0:T(8,128)(2,1)S(1)} %get-tuple-element.120) | copy-start | bytes 393220
  20.6 111.3 %all-reduce.16.cloned.1.call-start = ((), (), s32[]{:S(2)}) async-start(), calls=%async_computation.8 | async-start | bytes 524288 | tf_op jit(solution)/shard_map/psum | solution.py:103
  21.0 84.6 %copy-start.89 = (pred[128,1024]{1,0:T(8,128)(4,1)}, pred[128,1024]{1,0:T(8,128)(4,1)S(1)}, u32[]{:S(2)}) copy-start(pred[128,1024]{1,0:T(8,128)(4,1)S(1)} %iota_compare_fusion) | copy-start | bytes 393220
  69.6 39.1 %copy-start.137 = (f32[8,128]{1,0:T(8,128)}, f32[8,128]{1,0:T(8,128)S(1)}, u32[]{:S(2)}) copy-start(f32[8,128]{1,0:T(8,128)S(1)} %get-tuple-element.147) | copy-start | bytes 12292
  109.8 53.0 %all-reduce.18.cloned.1.call-start = ((), (), s32[]{:S(2)}) async-start(), calls=%async_computation.9 | async-start | bytes 524288 | tf_op jit(solution)/shard_map/psum | solution.py:114
  137.7 153.3 %copy-start.8 = (f32[128,2048]{1,0:T(8,128)}, f32[128,2048]{1,0:T(8,128)S(1)}, u32[]{:S(2)}) copy-start(f32[128,2048]{1,0:T(8,128)S(1)} %fusion.35) | copy-start | bytes 3145732
  139.4 73.9 %all-gather.19.cloned.1.call-start = ((), (), s32[]{:S(2)}) async-start(), calls=%async_computation.11 | async-start | bytes 1179648 | tf_op jit(solution)/shard_map/all_gather | solution.py:89
  163.9 2.4 collective-permute-start
  172.8 47.7 %copy-start.67 = (bf16[128,512]{1,0:T(8,128)(2,1)}, bf16[128,512]{1,0:T(8,128)(2,1)S(1)}, u32[]{:S(2)}) copy-start(bf16[128,512]{1,0:T(8,128)(2,1)S(1)} %get-tuple-element.119) | copy-start | bytes 393220
  172.8 81.4 %all-gather.17.cloned.1.call-start = ((), (), s32[]{:S(2)}) async-start(), calls=%async_computation.10 | async-start | bytes 1179648 | tf_op jit(solution)/shard_map/all_gather | solution.py:90
  173.4 109.8 %all-reduce.20.cloned.1.call-start = ((), (), s32[]{:S(2)}) async-start(), calls=%async_computation.12 | async-start | bytes 524288 | tf_op jit(solution)/shard_map/psum | solution.py:103
  260.0 193.3 %copy-start.58 = (bf16[128,8,64]{0,2,1:T(8,128)(2,1)}, bf16[128,8,64]{0,2,1:T(8,128)(2,1)S(1)}, u32[]{:S(2)}) copy-start(bf16[128,8,64]{0,2,1:T(8,128)(2,1)S(1)} %fusion.132) | copy-start | bytes 393220
  261.0 64.9 %all-reduce.34.cloned.1.call-start = ((), (), s32[]{:S(2)}) async-start(), calls=%async_computation.33 | async-start | bytes 1048576 | tf_op jit(solution)/shard_map/psum | solution.py:164
  297.1 37.9 %copy-start.68 = (bf16[128,512]{1,0:T(8,128)(2,1)S(1)}, bf16[128,512]{1,0:T(8,128)(2,1)}, u32[]{:S(2)}) copy-start(bf16[128,512]{1,0:T(8,128)(2,1)} %copy-done.67) | copy-start | bytes 393220
  297.1 71.8 %all-gather.25.cloned.1.call-start = ((), (), s32[]{:S(2)}) async-start(), calls=%async_computation.15 | async-start | bytes 1179648 | tf_op jit(solution)/shard_map/all_gather | solution.py:176
  297.8 112.1 %all-gather.23.cloned.1.call-start = ((), (), s32[]{:S(2)}) async-start(), calls=%async_computation.14 | async-start | bytes 1179648 | tf_op jit(solution)/shard_map/all_gather | solution.py:89
  327.8 43.4 %copy-start.76 = (bf16[128,1024]{1,0:T(8,128)(2,1)}, bf16[128,1024]{1,0:T(8,128)(2,1)S(1)}, u32[]{:S(2)}) copy-start(bf16[128,1024]{1,0:T(8,128)(2,1)S(1)} %get-tuple-element.85) | copy-start | bytes 786436
  327.8 2.7 collective-permute-start.1
  336.6 44.4 %copy-start.64 = (bf16[128,512]{1,0:T(8,128)(2,1)}, bf16[128,512]{1,0:T(8,128)(2,1)S(1)}, u32[]{:S(2)}) copy-start(bf16[128,512]{1,0:T(8,128)(2,1)S(1)} %get-tuple-element.113) | copy-start | bytes 393220
  336.6 38.7 %copy-start.77 = (bf16[128,1024]{1,0:T(8,128)(2,1)S(1)}, bf16[128,1024]{1,0:T(8,128)(2,1)}, u32[]{:S(2)}) copy-start(bf16[128,1024]{1,0:T(8,128)(2,1)} %get-tuple-element.74) | copy-start | bytes 786436
  336.6 114.4 %all-gather.27.cloned.1.call-start = ((), (), s32[]{:S(2)}) async-start(), calls=%async_computation.16 | async-start | bytes 1179648 | tf_op jit(solution)/shard_map/all_gather | solution.py:177
  337.4 154.7 %all-gather.21.cloned.1.call-start = ((), (), s32[]{:S(2)}) async-start(), calls=%async_computation.13 | async-start | bytes 1179648 | tf_op jit(solution)/shard_map/all_gather | solution.py:90
  375.2 183.8 %reduce-scatter.21.cloned.1.call-start = ((), (), s32[]{:S(2)}) async-start(), calls=%async_computation.25 | async-start | bytes 1179648
  378.2 281.4 %copy-start.29 = (f32[128,1024]{1,0:T(8,128)}, f32[128,1024]{1,0:T(8,128)S(1)}, u32[]{:S(2)}) copy-start(f32[128,1024]{1,0:T(8,128)S(1)} %get-tuple-element.79) | copy-start | bytes 1572868
  421.9 203.6 %reduce-scatter.19.cloned.1.call-start = ((), (), s32[]{:S(2)}) async-start(), calls=%async_computation.24 | async-start | bytes 1179648
  464.2 193.4 %all-reduce.32.cloned.1.call-start = ((), (), s32[]{:S(2)}) async-start(), calls=%async_computation.32 | async-start | bytes 1048576 | tf_op jit(solution)/shard_map/psum | solution.py:224
  500.4 162.6 %copy-start.54 = (bf16[8,64,128]{2,1,0:T(8,128)(2,1)}, bf16[8,64,128]{2,1,0:T(8,128)(2,1)S(1)}, u32[]{:S(2)}) copy-start(bf16[8,64,128]{2,1,0:T(8,128)(2,1)S(1)} %get-tuple-element.124) | copy-start | bytes 393220
  626.5 39.0 %copy-start.56 = (bf16[128,512]{0,1:T(8,128)(2,1)}, bf16[128,512]{0,1:T(8,128)(2,1)S(1)}, u32[]{:S(2)}) copy-start(bf16[128,512]{0,1:T(8,128)(2,1)S(1)} %copy.101) | copy-start | bytes 393220
  629.8 70.6 %all-gather.29.cloned.1.call-start = ((), (), s32[]{:S(2)}) async-start(), calls=%async_computation.18 | async-start | bytes 1179648 | tf_op jit(solution)/shard_map/all_gather | solution.py:176
  631.5 93.6 %all-reduce.22.cloned.1.call-start = ((), (), s32[]{:S(2)}) async-start(), calls=%async_computation.17 | async-start | bytes 524288 | tf_op jit(solution)/shard_map/psum | solution.py:164
  663.0 6.9 collective-permute-start.2
  675.4 92.1 %all-gather.31.cloned.1.call-start = ((), (), s32[]{:S(2)}) async-start(), calls=%async_computation.19 | async-start | bytes 1179648 | tf_op jit(solution)/shard_map/all_gather | solution.py:177
  676.1 132.5 %all-gather.33.cloned.1.call-start = ((), (), s32[]{:S(2)}) async-start(), calls=%async_computation.22 | async-start | bytes 1179648 | tf_op jit(solution)/shard_map/all_gather | solution.py:176
  676.2 49.0 %copy-start.7 = (bf16[128,1024]{1,0:T(8,128)(2,1)S(1)}, bf16[128,1024]{1,0:T(8,128)(2,1)}, u32[]{:S(2)}) copy-start(bf16[128,1024]{1,0:T(8,128)(2,1)} %get-tuple-element.73) | copy-start | bytes 786436
  676.2 49.0 %copy-start.113 = (f32[128]{0:T(128)S(1)}, f32[128]{0:T(128)}, u32[]{:S(2)}) copy-start(f32[128]{0:T(128)} %copy-done.111) | copy-start | bytes 1540
  676.2 49.0 %copy-start.118 = (f32[128]{0:T(128)S(1)}, f32[128]{0:T(128)}, u32[]{:S(2)}) copy-start(f32[128]{0:T(128)} %copy-done.116) | copy-start | bytes 1540
  676.2 49.0 %copy-start.120 = (f32[128]{0:T(128)S(1)}, f32[128]{0:T(128)}, u32[]{:S(2)}) copy-start(f32[128]{0:T(128)} %copy-done.119) | copy-start | bytes 1540
  676.2 49.0 %copy-start.126 = (f32[128]{0:T(128)S(1)}, f32[128]{0:T(128)}, u32[]{:S(2)}) copy-start(f32[128]{0:T(128)} %copy-done.125) | copy-start | bytes 1540
  676.9 172.7 %all-gather.35.cloned.1.call-start = ((), (), s32[]{:S(2)}) async-start(), calls=%async_computation.23 | async-start | bytes 1179648 | tf_op jit(solution)/shard_map/all_gather | solution.py:177
  677.1 50.2 %copy-start.70 = (bf16[128,512]{0,1:T(8,128)(2,1)}, bf16[128,512]{0,1:T(8,128)(2,1)S(1)}, u32[]{:S(2)}) copy-start(bf16[128,512]{0,1:T(8,128)(2,1)S(1)} %copy.91) | copy-start | bytes 393220
  677.5 238.5 %reduce-scatter.25.cloned.1.call-start = ((), (), s32[]{:S(2)}) async-start(), calls=%async_computation.27 | async-start | bytes 1179648
  738.7 243.9 %reduce-scatter.23.cloned.1.call-start = ((), (), s32[]{:S(2)}) async-start(), calls=%async_computation.26 | async-start | bytes 1179648
  780.6 229.5 %all-reduce.24.cloned.1.call-start = ((), (), s32[]{:S(2)}) async-start(), calls=%async_computation.20 | async-start | bytes 524288 | tf_op jit(solution)/shard_map/psum | solution.py:224
  987.7 63.3 %all-reduce.26.cloned.1.call-start = ((), (), s32[]{:S(2)}) async-start(), calls=%async_computation.21 | async-start | bytes 524288 | tf_op jit(solution)/shard_map/psum | solution.py:164
  1015.3 5.3 collective-permute-start.3
  1026.7 102.7 %reduce-scatter.29.cloned.1.call-start = ((), (), s32[]{:S(2)}) async-start(), calls=%async_computation.29 | async-start | bytes 1179648
  1065.1 130.8 %reduce-scatter.27.cloned.1.call-start = ((), (), s32[]{:S(2)}) async-start(), calls=%async_computation.28 | async-start | bytes 1179648
  1084.3 143.6 %all-reduce.30.cloned.1.call-start = ((), (), s32[]{:S(2)}) async-start(), calls=%async_computation.31 | async-start | bytes 1048576 | tf_op jit(solution)/shard_map/psum | solution.py:114
  1105.7 94.6 %copy-start.99 = (f32[128]{0:T(128)S(1)}, f32[128]{0:T(128)}, u32[]{:S(2)}) copy-start(f32[128]{0:T(128)} %copy-done.98) | copy-start | bytes 1540
  1105.7 94.6 %copy-start.103 = (f32[128]{0:T(128)S(1)}, f32[128]{0:T(128)}, u32[]{:S(2)}) copy-start(f32[128]{0:T(128)} %copy-done.101) | copy-start | bytes 1540
  1105.7 94.6 %copy-start.106 = (f32[128]{0:T(128)S(1)}, f32[128]{0:T(128)}, u32[]{:S(2)}) copy-start(f32[128]{0:T(128)} %copy-done.104) | copy-start | bytes 1540
  1105.7 94.6 %copy-start.110 = (f32[128]{0:T(128)S(1)}, f32[128]{0:T(128)}, u32[]{:S(2)}) copy-start(f32[128]{0:T(128)} %copy-done.109) | copy-start | bytes 1540
  1130.5 77.3 %copy-start.48 = (bf16[128,512]{0,1:T(8,128)(2,1)}, bf16[128,512]{0,1:T(8,128)(2,1)S(1)}, u32[]{:S(2)}) copy-start(bf16[128,512]{0,1:T(8,128)(2,1)S(1)} %copy.111) | copy-start | bytes 393220
  1200.2 428.9 %all-reduce.28.cloned.1.call-start = ((), (), s32[]{:S(2)}) async-start(), calls=%async_computation.30 | async-start | bytes 25165824 | tf_op jit(solution)/shard_map/psum | solution.py:316
  1212.4 61.5 %copy-start.95 = (f32[1,1024]{1,0:T(1,128)S(1)}, f32[1,1024]{1,0:T(1,128)}, u32[]{:S(2)}) copy-start(f32[1,1024]{1,0:T(1,128)} %copy-done.93) | copy-start | bytes 12292
  1213.5 63.5 %copy-start.34 = (f32[128,1024]{1,0:T(8,128)S(1)}, f32[128,1024]{1,0:T(8,128)}, u32[]{:S(2)}) copy-start(f32[128,1024]{1,0:T(8,128)} %copy-done.33) | copy-start | bytes 1572868
  1214.1 64.1 %copy-start.49 = (f32[1,128,1024]{2,1,0:T(8,128)S(1)}, f32[1,128,1024]{2,1,0:T(8,128)}, u32[]{:S(2)}) copy-start(f32[1,128,1024]{2,1,0:T(8,128)} %get-tuple-element.82) | copy-start | bytes 1572868
  (121 other events, 1137.3 us)
Sparse Core Ops, SparseCore 0:
  19.9 42.9 all-gather.14
  65.1 38.9 all-gather.12
  109.9 21.9 all-reduce.15
  139.5 23.2 all-reduce.17
  173.0 40.2 all-gather.18
  215.3 38.9 all-gather.16
  261.2 21.9 all-reduce.19
  297.2 28.6 all-reduce.33
  328.6 40.2 all-gather.24
  370.9 38.9 all-gather.22
  412.0 38.9 all-gather.26
  453.0 38.9 all-gather.20
  496.0 62.9 reduce-scatter.20
  562.3 63.1 reduce-scatter.18
  629.9 27.6 all-reduce.31
  660.1 40.2 all-gather.28
  703.1 21.9 all-reduce.21
  727.1 40.2 all-gather.30
  769.6 38.9 all-gather.32
  810.6 38.9 all-gather.34
  853.0 62.8 reduce-scatter.24
  919.3 63.2 reduce-scatter.22
  987.8 22.3 all-reduce.23
  1026.8 24.0 all-reduce.25
  1065.2 64.1 reduce-scatter.28
  1132.7 63.1 reduce-scatter.26
  1200.3 27.6 all-reduce.29
  1233.9 395.0 all-reduce.27
where the time goes:
time: 1670 us; the launch traced here: 1660 us
  waiting for transfers between devices  1240 us (74%)
  matrix products  188 us (11%)
  local copies, waits for them, and re-layouts  87.3 us (5%)
  other arithmetic  77.7 us (5%)
  blocking collectives  39.5 us (2%)
    psum x1, waiting for transfers between devices, body(): lax.psum(grad_totals[0].astype(jnp.bfloat16), 'ctx').astype(jnp.float32)  350 us
    unnamed x34, waiting for transfers between devices  338 us
    all_gather x3, waiting for transfers between devices, layer_forward(): lax.all_gather(key_rows, 'ctx', axis=0, tiled=True)  110 us
    all_gather x3, waiting for transfers between devices, layer_backward(): lax.all_gather(held_keys[1], 'ctx', axis=0, tiled=True)  96.4 us
    all_gather x3, waiting for transfers between devices, layer_forward(): lax.all_gather(val_rows, 'ctx', axis=0, tiled=True)  96 us
    all_gather x3, waiting for transfers between devices, layer_backward(): lax.all_gather(held_keys[0], 'ctx', axis=0, tiled=True)  66.6 us
    psum x3, waiting for transfers between devices, layer_backward(): lax.psum(jnp.dot(d_pre_bf, w_fc.T, preferred_element_type=jnp.float32).as...  64.1 us
    psum x2, waiting for transfers between devices, layer_forward(): lax.psum(jnp.dot(attended, w_out, preferred_element_type=jnp.float32).ast...  43.7 us
  transfers between devices with their start and end apart: 32, of which 30 were waited for; matrix products, arithmetic and copies ran while one was open for 14% of the time, Pallas kernels for 0%

commit v1 on v0

--- a/solution.py
+++ b/solution.py
@@ -313,7 +313,9 @@
         ]
     )[None]
     summed = (
-        lax.psum(grad_totals[0].astype(jnp.bfloat16), "ctx").astype(jnp.float32),
+        jnp.sum(lax.all_gather(grad_totals[0].astype(jnp.bfloat16), "ctx"), axis=0).astype(
+            jnp.float32
+        ),
         lax.psum(grad_totals[1].astype(jnp.bfloat16), "ctx").astype(jnp.float32),
         lax.psum(grad_totals[2].astype(jnp.bfloat16), "ctx").astype(jnp.float32),
         lax.psum(grad_totals[3].astype(jnp.bfloat16), "ctx").astype(jnp.float32),

time: 1670 us -> 2040 us (1.22)
  waiting for transfers between devices: 1240 us -> 1600 us
    all_gather x0 -> x1, waiting for transfers between devices: none -> 467 us  [body(): lax.all_gather(grad_totals[0].astype(jnp.bfloat16), 'ctx')]
    psum x1, waiting for transfers between devices: 350 us -> 249 us  [body(): lax.psum(grad_totals[2].astype(jnp.bfloat16), 'ctx').astype(jnp.float32)]
    psum x3 -> x2, waiting for transfers between devices: 64.1 us -> 37 us  [layer_backward(): lax.psum(jnp.dot(d_pre_bf, w_fc.T, preferred_element_type=jnp.float32).as...]
    psum x2 -> x3, waiting for transfers between devices: 43.7 us -> 69.7 us  [layer_forward(): lax.psum(jnp.dot(attended, w_out, preferred_element_type=jnp.float32).ast...]
    psum x2 -> x3, waiting for transfers between devices: 28.7 us -> 51.4 us  [layer_forward(): lax.psum(jnp.dot(act_bf, w_proj, preferred_element_type=jnp.float32).asty...]
    psum x2 -> x1, waiting for transfers between devices: 43.1 us -> 21.7 us  [layer_backward(): lax.psum(jnp.dot(d_joined, w_qkv.reshape(model_width, 3 * local_cols).T,...]
    unnamed x34 -> x35, waiting for transfers between devices: 338 us -> 345 us
    unnamed x320 -> x349, local copies, waits for them, and re-layouts: 42.3 us -> 46.1 us
  transfers between devices with their start and end apart: 32 -> 33, of which waited for: 30 -> 31; matrix products, arithmetic and copies ran while one was open for 14% -> 13% of each run, Pallas kernels for 0% -> 0%
where the time goes in v1:
time: 2040 us; the launch traced here: 2030 us
  waiting for transfers between devices  1600 us (78%)
  matrix products  171 us (8%)
  other arithmetic  96.9 us (5%)
  local copies, waits for them, and re-layouts  96.2 us (5%)
  blocking collectives  37.3 us (2%)
    all_gather x1, waiting for transfers between devices, body(): lax.all_gather(grad_totals[0].astype(jnp.bfloat16), 'ctx')  467 us
    unnamed x35, waiting for transfers between devices  345 us
    psum x1, waiting for transfers between devices, body(): lax.psum(grad_totals[2].astype(jnp.bfloat16), 'ctx').astype(jnp.float32)  249 us
    all_gather x3, waiting for transfers between devices, layer_forward(): lax.all_gather(key_rows, 'ctx', axis=0, tiled=True)  109 us
    all_gather x3, waiting for transfers between devices, layer_forward(): lax.all_gather(val_rows, 'ctx', axis=0, tiled=True)  96.6 us
    all_gather x3, waiting for transfers between devices, layer_backward(): lax.all_gather(held_keys[1], 'ctx', axis=0, tiled=True)  79.5 us
    psum x3, waiting for transfers between devices, layer_forward(): lax.psum(jnp.dot(attended, w_out, preferred_element_type=jnp.float32).ast...  69.7 us
    all_gather x3, waiting for transfers between devices, layer_backward(): lax.all_gather(held_keys[0], 'ctx', axis=0, tiled=True)  69 us
  transfers between devices with their start and end apart: 33, of which 31 were waited for; matrix products, arithmetic and copies ran while one was open for 13% of the time, Pallas kernels for 0%

profile of v1, /device:TPU:0, one launch (start us, length us, event | category | flops | bytes accessed | tf_op | source)
XLA Modules:
  0.0 2026.5 jit_solution(13351605243480563858)
XLA Ops:
  11.3 4.7 copy.74
  21.0 42.0 %all-gather.16.cloned.1.call-done = bf16[1024,512]{1,0:T(8,128)(2,1)} async-done(((bf16[128,512]{1,0:T(8,128)(2,1)}), bf16[1024,512]{1,0:T(8,128)(2,1)}) %all-gather.16.cloned.1.call-update) | async-done | bytes 1048592 | tf_op jit(solution)/shard_map/all_gather | solution.py:89
  65.2 4.4 fusion.24
  69.6 34.5 %all-gather.14.cloned.1.call-done = bf16[1024,512]{1,0:T(8,128)(2,1)} async-done(((bf16[128,512]{1,0:T(8,128)(2,1)}), bf16[1024,512]{1,0:T(8,128)(2,1)}) %all-gather.14.cloned.1.call-update) | async-done | bytes 1048592 | tf_op jit(solution)/shard_map/all_gather | solution.py:90
  109.9 22.1 %all-reduce.16.cloned.1.call-done = bf16[128,1024]{1,0:T(8,128)(2,1)} async-done(((bf16[128,1024]{1,0:T(8,128)(2,1)}), bf16[128,1024]{1,0:T(8,128)(2,1)}) %all-reduce.16.cloned.1.call-update) | async-done | bytes 262160 | tf_op jit(solution)/shard_map/psum | solution.py:103
  134.5 3.1 fusion.35
  139.4 23.4 %all-reduce.18.cloned.1.call-done = bf16[128,1024]{1,0:T(8,128)(2,1)} async-done(((bf16[128,1024]{1,0:T(8,128)(2,1)}), bf16[128,1024]{1,0:T(8,128)(2,1)}) %all-reduce.18.cloned.1.call-update) | async-done | bytes 262160 | tf_op jit(solution)/shard_map/psum | solution.py:114
  174.3 39.0 %all-gather.20.cloned.1.call-done = bf16[1024,512]{1,0:T(8,128)(2,1)} async-done(((bf16[128,512]{1,0:T(8,128)(2,1)}), bf16[1024,512]{1,0:T(8,128)(2,1)}) %all-gather.20.cloned.1.call-update) | async-done | bytes 1048592 | tf_op jit(solution)/shard_map/all_gather | solution.py:89
  215.6 4.5 fusion.26
  220.0 34.3 %all-gather.18.cloned.1.call-done = bf16[1024,512]{1,0:T(8,128)(2,1)} async-done(((bf16[128,512]{1,0:T(8,128)(2,1)}), bf16[1024,512]{1,0:T(8,128)(2,1)}) %all-gather.18.cloned.1.call-update) | async-done | bytes 1048592 | tf_op jit(solution)/shard_map/all_gather | solution.py:90
  256.6 3.4 fusion.132
  261.6 21.6 %all-reduce.20.cloned.1.call-done = bf16[128,1024]{1,0:T(8,128)(2,1)} async-done(((bf16[128,1024]{1,0:T(8,128)(2,1)}), bf16[128,1024]{1,0:T(8,128)(2,1)}) %all-reduce.20.cloned.1.call-update) | async-done | bytes 262160 | tf_op jit(solution)/shard_map/psum | solution.py:103
  297.9 28.0 %all-reduce.34.cloned.1.call-done = (bf16[128,1024]{1,0:T(8,128)(2,1)}, bf16[128,1024]{1,0:T(8,128)(2,1)}) async-done(((bf16[128,1024]{1,0:T(8,128)(2,1)}, bf16[128,1024]{1,0:T(8,128)(2,1)}), (bf16[128,1024]{1,0:T(8,128)(2,1)}, bf16[128,1024]{1,0:T(8,128)(2,1)})) %all-reduce.34.cloned.1.call-update) | async-done | bytes 524304 | tf_op jit(solution)/shard_map/psum | solution.py:114
  338.6 30.3 %all-gather.26.cloned.1.call-done = bf16[1024,512]{1,0:T(8,128)(2,1)} async-done(((bf16[128,512]{1,0:T(8,128)(2,1)}), bf16[1024,512]{1,0:T(8,128)(2,1)}) %all-gather.26.cloned.1.call-update) | async-done | bytes 1048592 | tf_op jit(solution)/shard_map/all_gather | solution.py:176
  371.2 4.0 fusion.384
  381.8 28.1 %all-gather.24.cloned.1.call-done = bf16[1024,512]{1,0:T(8,128)(2,1)} async-done(((bf16[128,512]{1,0:T(8,128)(2,1)}), bf16[1024,512]{1,0:T(8,128)(2,1)}) %all-gather.24.cloned.1.call-update) | async-done | bytes 1048592 | tf_op jit(solution)/shard_map/all_gather | solution.py:89
  412.2 4.6 fusion.28
  422.1 29.0 %all-gather.28.cloned.1.call-done = bf16[1024,512]{1,0:T(8,128)(2,1)} async-done(((bf16[128,512]{1,0:T(8,128)(2,1)}), bf16[1024,512]{1,0:T(8,128)(2,1)}) %all-gather.28.cloned.1.call-update) | async-done | bytes 1048592 | tf_op jit(solution)/shard_map/all_gather | solution.py:177
  455.0 4.2 multiply_convert_fusion.2
  464.3 27.8 %all-gather.22.cloned.1.call-done = bf16[1024,512]{1,0:T(8,128)(2,1)} async-done(((bf16[128,512]{1,0:T(8,128)(2,1)}), bf16[1024,512]{1,0:T(8,128)(2,1)}) %all-gather.22.cloned.1.call-update) | async-done | bytes 1048592 | tf_op jit(solution)/shard_map/all_gather | solution.py:90
  494.4 3.5 fusion.126
  500.5 58.0 %reduce-scatter.21.cloned.1.call-done = bf16[128,512]{1,0:T(8,128)(2,1)} async-done(((bf16[1024,512]{1,0:T(8,128)(2,1)}), bf16[128,512]{1,0:T(8,128)(2,1)}) %reduce-scatter.21.cloned.1.call-update) | async-done | bytes 131088
  559.5 66.0 %reduce-scatter.19.cloned.1.call-done = bf16[128,512]{1,0:T(8,128)(2,1)} async-done(((bf16[1024,512]{1,0:T(8,128)(2,1)}), bf16[128,512]{1,0:T(8,128)(2,1)}) %reduce-scatter.19.cloned.1.call-update) | async-done | bytes 131088
  626.6 3.3 convolution_convert_fusion.2
  631.6 26.0 %all-reduce.32.cloned.1.call-done = (bf16[128,1024]{1,0:T(8,128)(2,1)}, bf16[128,1024]{1,0:T(8,128)(2,1)}) async-done(((bf16[128,1024]{1,0:T(8,128)(2,1)}, bf16[128,1024]{1,0:T(8,128)(2,1)}), (bf16[128,1024]{1,0:T(8,128)(2,1)}, bf16[128,1024]{1,0:T(8,128)(2,1)})) %all-reduce.32.cloned.1.call-update) | async-done | bytes 524304 | tf_op jit(solution)/shard_map/psum | solution.py:103
  666.7 3.2 fusion.41
  678.2 22.3 %all-gather.30.cloned.1.call-done = bf16[1024,512]{1,0:T(8,128)(2,1)} async-done(((bf16[128,512]{1,0:T(8,128)(2,1)}), bf16[1024,512]{1,0:T(8,128)(2,1)}) %all-gather.30.cloned.1.call-update) | async-done | bytes 1048592 | tf_op jit(solution)/shard_map/all_gather | solution.py:176
  702.7 4.0 fusion.385
  706.7 18.5 all-reduce.22.cloned.1.call-done
  732.0 4.3 fusion.89
  738.7 28.8 %all-gather.32.cloned.1.call-done = bf16[1024,512]{1,0:T(8,128)(2,1)} async-done(((bf16[128,512]{1,0:T(8,128)(2,1)}), bf16[1024,512]{1,0:T(8,128)(2,1)}) %all-gather.32.cloned.1.call-update) | async-done | bytes 1048592 | tf_op jit(solution)/shard_map/all_gather | solution.py:177
  771.4 4.2 multiply_convert_fusion.1
  780.8 4.0 fusion.377
  784.8 49.6 %reduce-scatter.25.cloned.1.call-done = bf16[128,512]{1,0:T(8,128)(2,1)} async-done(((bf16[1024,512]{1,0:T(8,128)(2,1)}), bf16[128,512]{1,0:T(8,128)(2,1)}) %reduce-scatter.25.cloned.1.call-update) | async-done | bytes 131088
  836.0 64.8 %reduce-scatter.23.cloned.1.call-done = bf16[128,512]{1,0:T(8,128)(2,1)} async-done(((bf16[1024,512]{1,0:T(8,128)(2,1)}), bf16[128,512]{1,0:T(8,128)(2,1)}) %reduce-scatter.23.cloned.1.call-update) | async-done | bytes 131088
  902.5 3.4 convolution_convert_fusion.1
  906.7 21.7 %all-reduce.24.cloned.1.call-done = bf16[128,1024]{1,0:T(8,128)(2,1)} async-done(((bf16[128,1024]{1,0:T(8,128)(2,1)}), bf16[128,1024]{1,0:T(8,128)(2,1)}) %all-reduce.24.cloned.1.call-update) | async-done | bytes 262160 | tf_op jit(solution)/shard_map/psum | solution.py:224
  937.3 5.5 fusion.381
  946.3 6.5 fusion.245
  954.5 16.4 all-gather.34.cloned.1.call-done
  973.1 4.1 fusion.386
  977.2 18.5 all-reduce.26.cloned.1.call-done
  1002.7 4.4 fusion.92
  1009.5 4.9 fusion.275
  1016.2 21.8 %all-gather.36.cloned.1.call-done = bf16[1024,512]{1,0:T(8,128)(2,1)} async-done(((bf16[128,512]{1,0:T(8,128)(2,1)}), bf16[1024,512]{1,0:T(8,128)(2,1)}) %all-gather.36.cloned.1.call-update) | async-done | bytes 1048592 | tf_op jit(solution)/shard_map/all_gather | solution.py:177
  1040.3 3.9 fusion.111
  1050.2 6.1 fusion.273
  1059.8 3.6 fusion.31
  1063.4 3.2 fusion.378
  1066.6 37.9 %reduce-scatter.29.cloned.1.call-done = bf16[128,512]{1,0:T(8,128)(2,1)} async-done(((bf16[1024,512]{1,0:T(8,128)(2,1)}), bf16[128,512]{1,0:T(8,128)(2,1)}) %reduce-scatter.29.cloned.1.call-update) | async-done | bytes 131088
  1105.5 66.0 %reduce-scatter.27.cloned.1.call-done = bf16[128,512]{1,0:T(8,128)(2,1)} async-done(((bf16[1024,512]{1,0:T(8,128)(2,1)}), bf16[128,512]{1,0:T(8,128)(2,1)}) %reduce-scatter.27.cloned.1.call-update) | async-done | bytes 131088
  1172.5 3.2 convolution_convert_fusion
  1175.9 9.6 fusion.30
  1193.4 4.7 copy.96
  1198.1 4.7 copy.97
  1211.2 37.3 %all-reduce = (bf16[1,2,512]{2,1,0:T(2,128)(2,1)S(1)}, bf16[1,1024]{1,0:T(2,128)(2,1)S(1)}, bf16[1,2048]{1,0:T(2,128)(2,1)S(1)}, bf16[1,1024]{1,0:T(2,128)(2,1)S...) all-reduce(bf16[1,2,512]{2,1,0:T(2,128)(2,1)S(1)} %fusion.327, ...), channel_id=1, replica_groups=mesh['section'=2,'ctx'=8,'tp'=2] {'ctx'}, use_global_device_ids=true, to_apply=%region_55.56 | all-reduce | flops 9216 | bytes 36864 | tf_op jit(solution)/shard_map/psum | solution.py:319
  1257.5 249.4 %all-reduce.28.cloned.1.call-done = (bf16[1,512,1024]{2,1,0:T(8,128)(2,1)}, bf16[1,1024,2048]{2,1,0:T(8,128)(2,1)}, bf16[1,2048,1024]{2,1,0:T(8,128)(2,1)}) async-done(((bf16[1,512,1024]{2,1,0:T(8,128)(2,1)}, bf16[1,1024,2048]{2,1,0:T(8,128)(2,1)}, bf16[1,2048,1024]{2,1,0:T(8,128)(2,1)}), (bf16[1,512,1024]{2,1,0:T(8,128)(2,1)}, bf16[1,1024,2048]{2,1,0:T(8,128)(2,1)}, ...) | async-done | bytes 9437200 | tf_op jit(solution)/shard_map/psum | solution.py:320
  1509.8 7.1 broadcast_in_dim.170
  1516.9 4.4 broadcast_in_dim.174
  1521.3 466.6 %all-gather.38.cloned.1.call-done = bf16[8,1024,3,512]{3,1,2,0:T(8,128)(2,1)} async-done(((bf16[1,1024,3,512]{3,1,2,0:T(8,128)(2,1)}), bf16[8,1024,3,512]{3,1,2,0:T(8,128)(2,1)}) %all-gather.38.cloned.1.call-update) | async-done | bytes 25165840 | tf_op jit(solution)/shard_map/all_gather | solution.py:316
  1987.9 15.3 reduce_sum.555
  2003.2 4.7 copy.112
  2007.9 5.4 bitcast_convert_fusion
  2013.2 6.6 copy.99
  (561 shorter events, 210.1 us)
Async XLA Ops:
  7.2 101.6 %copy-start = (bf16[1,512,1024]{2,1,0:T(8,128)(2,1)S(1)}, bf16[1,512,1024]{2,1,0:T(8,128)(2,1)}, u32[]{:S(2)}) copy-start(bf16[1,512,1024]{2,1,0:T(8,128)(2,1)} %param.16) | copy-start | bytes 3145732
  7.2 55.8 %all-gather.16.cloned.1.call-start = ((), (), s32[]{:S(2)}) async-start(), calls=%async_computation.7 | async-start | bytes 1179648 | tf_op jit(solution)/shard_map/all_gather | solution.py:89
  11.2 123.3 %copy-start.86 = (f32[1,1,1024]{2,1,0:T(1,128)}, f32[1,1,1024]{2,1,0:T(1,128)S(1)}, u32[]{:S(2)}) copy-start(f32[1,1,1024]{2,1,0:T(1,128)S(1)} %get-tuple-element.119) | copy-start | bytes 12292
  19.1 50.6 %copy-start.36 = (f32[128,1536]{1,0:T(8,128)}, f32[128,1536]{1,0:T(8,128)S(1)}, u32[]{:S(2)}) copy-start(f32[128,1536]{1,0:T(8,128)S(1)} %fusion.264) | copy-start | bytes 2359300
  19.8 84.3 %all-gather.14.cloned.1.call-start = ((), (), s32[]{:S(2)}) async-start(), calls=%async_computation.6 | async-start | bytes 1179648 | tf_op jit(solution)/shard_map/all_gather | solution.py:90
  19.9 49.7 %copy-start.123 = (f32[1,1,512]{2,1,0:T(1,128)}, f32[1,1,512]{2,1,0:T(1,128)S(1)}, u32[]{:S(2)}) copy-start(f32[1,1,512]{2,1,0:T(1,128)S(1)} %get-tuple-element.123) | copy-start | bytes 6148
  19.9 49.7 %copy-start.124 = (f32[1,1,512]{2,1,0:T(1,128)}, f32[1,1,512]{2,1,0:T(1,128)S(1)}, u32[]{:S(2)}) copy-start(f32[1,1,512]{2,1,0:T(1,128)S(1)} %get-tuple-element.124) | copy-start | bytes 6148
  20.6 150.4 %copy-start.52 = (bf16[128,512]{1,0:T(8,128)(2,1)}, bf16[128,512]{1,0:T(8,128)(2,1)S(1)}, u32[]{:S(2)}) copy-start(bf16[128,512]{1,0:T(8,128)(2,1)S(1)} %get-tuple-element.107) | copy-start | bytes 393220
  20.6 111.3 %all-reduce.16.cloned.1.call-start = ((), (), s32[]{:S(2)}) async-start(), calls=%async_computation.8 | async-start | bytes 524288 | tf_op jit(solution)/shard_map/psum | solution.py:103
  21.0 84.6 %copy-start.98 = (pred[128,1024]{1,0:T(8,128)(4,1)}, pred[128,1024]{1,0:T(8,128)(4,1)S(1)}, u32[]{:S(2)}) copy-start(pred[128,1024]{1,0:T(8,128)(4,1)S(1)} %iota_compare_fusion) | copy-start | bytes 393220
  109.8 53.0 %all-reduce.18.cloned.1.call-start = ((), (), s32[]{:S(2)}) async-start(), calls=%async_computation.9 | async-start | bytes 524288 | tf_op jit(solution)/shard_map/psum | solution.py:114
  137.7 153.3 %copy-start.9 = (f32[128,2048]{1,0:T(8,128)}, f32[128,2048]{1,0:T(8,128)S(1)}, u32[]{:S(2)}) copy-start(f32[128,2048]{1,0:T(8,128)S(1)} %fusion.35) | copy-start | bytes 3145732
  139.4 73.9 %all-gather.20.cloned.1.call-start = ((), (), s32[]{:S(2)}) async-start(), calls=%async_computation.11 | async-start | bytes 1179648 | tf_op jit(solution)/shard_map/all_gather | solution.py:89
  164.0 2.4 collective-permute-start
  172.8 47.2 %copy-start.71 = (bf16[128,512]{1,0:T(8,128)(2,1)}, bf16[128,512]{1,0:T(8,128)(2,1)S(1)}, u32[]{:S(2)}) copy-start(bf16[128,512]{1,0:T(8,128)(2,1)S(1)} %get-tuple-element.106) | copy-start | bytes 393220
  172.9 81.4 %all-gather.18.cloned.1.call-start = ((), (), s32[]{:S(2)}) async-start(), calls=%async_computation.10 | async-start | bytes 1179648 | tf_op jit(solution)/shard_map/all_gather | solution.py:90
  173.5 109.8 %all-reduce.20.cloned.1.call-start = ((), (), s32[]{:S(2)}) async-start(), calls=%async_computation.12 | async-start | bytes 524288 | tf_op jit(solution)/shard_map/psum | solution.py:103
  260.0 193.3 %copy-start.62 = (bf16[128,8,64]{0,2,1:T(8,128)(2,1)}, bf16[128,8,64]{0,2,1:T(8,128)(2,1)S(1)}, u32[]{:S(2)}) copy-start(bf16[128,8,64]{0,2,1:T(8,128)(2,1)S(1)} %fusion.132) | copy-start | bytes 393220
  261.1 64.8 %all-reduce.34.cloned.1.call-start = ((), (), s32[]{:S(2)}) async-start(), calls=%async_computation.34 | async-start | bytes 1048576 | tf_op jit(solution)/shard_map/psum | solution.py:114
  297.1 71.8 %all-gather.26.cloned.1.call-start = ((), (), s32[]{:S(2)}) async-start(), calls=%async_computation.15 | async-start | bytes 1179648 | tf_op jit(solution)/shard_map/all_gather | solution.py:176
  297.9 112.1 %all-gather.24.cloned.1.call-start = ((), (), s32[]{:S(2)}) async-start(), calls=%async_computation.14 | async-start | bytes 1179648 | tf_op jit(solution)/shard_map/all_gather | solution.py:89
  327.8 2.7 collective-permute-start.1
  336.8 44.3 %copy-start.68 = (bf16[128,512]{1,0:T(8,128)(2,1)}, bf16[128,512]{1,0:T(8,128)(2,1)S(1)}, u32[]{:S(2)}) copy-start(bf16[128,512]{1,0:T(8,128)(2,1)S(1)} %get-tuple-element.100) | copy-start | bytes 393220
  336.8 114.3 %all-gather.28.cloned.1.call-start = ((), (), s32[]{:S(2)}) async-start(), calls=%async_computation.16 | async-start | bytes 1179648 | tf_op jit(solution)/shard_map/all_gather | solution.py:177
  337.5 154.6 %all-gather.22.cloned.1.call-start = ((), (), s32[]{:S(2)}) async-start(), calls=%async_computation.13 | async-start | bytes 1179648 | tf_op jit(solution)/shard_map/all_gather | solution.py:90
  375.3 183.2 %reduce-scatter.21.cloned.1.call-start = ((), (), s32[]{:S(2)}) async-start(), calls=%async_computation.26 | async-start | bytes 1179648
  378.2 281.3 %copy-start.27 = (f32[128,1024]{1,0:T(8,128)}, f32[128,1024]{1,0:T(8,128)S(1)}, u32[]{:S(2)}) copy-start(f32[128,1024]{1,0:T(8,128)S(1)} %get-tuple-element.66) | copy-start | bytes 1572868
  421.9 203.6 %reduce-scatter.19.cloned.1.call-start = ((), (), s32[]{:S(2)}) async-start(), calls=%async_computation.25 | async-start | bytes 1179648
  464.2 193.4 %all-reduce.32.cloned.1.call-start = ((), (), s32[]{:S(2)}) async-start(), calls=%async_computation.33 | async-start | bytes 1048576 | tf_op jit(solution)/shard_map/psum | solution.py:103
  500.5 162.5 %copy-start.54 = (bf16[8,64,128]{2,1,0:T(8,128)(2,1)}, bf16[8,64,128]{2,1,0:T(8,128)(2,1)S(1)}, u32[]{:S(2)}) copy-start(bf16[8,64,128]{2,1,0:T(8,128)(2,1)S(1)} %get-tuple-element.111) | copy-start | bytes 393220
  629.8 70.6 %all-gather.30.cloned.1.call-start = ((), (), s32[]{:S(2)}) async-start(), calls=%async_computation.18 | async-start | bytes 1179648 | tf_op jit(solution)/shard_map/all_gather | solution.py:176
  631.6 93.6 %all-reduce.22.cloned.1.call-start = ((), (), s32[]{:S(2)}) async-start(), calls=%async_computation.17 | async-start | bytes 524288 | tf_op jit(solution)/shard_map/psum | solution.py:164
  663.0 6.9 collective-permute-start.2
  675.4 92.1 %all-gather.32.cloned.1.call-start = ((), (), s32[]{:S(2)}) async-start(), calls=%async_computation.19 | async-start | bytes 1179648 | tf_op jit(solution)/shard_map/all_gather | solution.py:177
  676.1 49.1 %copy-start.8 = (bf16[128,1024]{1,0:T(8,128)(2,1)S(1)}, bf16[128,1024]{1,0:T(8,128)(2,1)}, u32[]{:S(2)}) copy-start(bf16[128,1024]{1,0:T(8,128)(2,1)} %get-tuple-element.59) | copy-start | bytes 786436
  676.1 49.1 %copy-start.121 = (f32[128]{0:T(128)S(1)}, f32[128]{0:T(128)}, u32[]{:S(2)}) copy-start(f32[128]{0:T(128)} %copy-done.119) | copy-start | bytes 1540
  676.1 49.1 %copy-start.127 = (f32[128]{0:T(128)S(1)}, f32[128]{0:T(128)}, u32[]{:S(2)}) copy-start(f32[128]{0:T(128)} %copy-done.125) | copy-start | bytes 1540
  676.1 49.1 %copy-start.130 = (f32[128]{0:T(128)S(1)}, f32[128]{0:T(128)}, u32[]{:S(2)}) copy-start(f32[128]{0:T(128)} %copy-done.129) | copy-start | bytes 1540
  676.1 49.1 %copy-start.137 = (f32[128]{0:T(128)S(1)}, f32[128]{0:T(128)}, u32[]{:S(2)}) copy-start(f32[128]{0:T(128)} %copy-done.136) | copy-start | bytes 1540
  677.2 50.1 %copy-start.74 = (bf16[128,512]{0,1:T(8,128)(2,1)}, bf16[128,512]{0,1:T(8,128)(2,1)S(1)}, u32[]{:S(2)}) copy-start(bf16[128,512]{0,1:T(8,128)(2,1)S(1)} %copy.89) | copy-start | bytes 393220
  677.9 156.5 %reduce-scatter.25.cloned.1.call-start = ((), (), s32[]{:S(2)}) async-start(), calls=%async_computation.28 | async-start | bytes 1179648
  738.7 162.1 %reduce-scatter.23.cloned.1.call-start = ((), (), s32[]{:S(2)}) async-start(), calls=%async_computation.27 | async-start | bytes 1179648
  780.7 147.7 %all-reduce.24.cloned.1.call-start = ((), (), s32[]{:S(2)}) async-start(), calls=%async_computation.20 | async-start | bytes 524288 | tf_op jit(solution)/shard_map/psum | solution.py:224
  905.9 64.9 %all-gather.34.cloned.1.call-start = ((), (), s32[]{:S(2)}) async-start(), calls=%async_computation.22 | async-start | bytes 1179648 | tf_op jit(solution)/shard_map/all_gather | solution.py:176
  906.7 89.1 %all-reduce.26.cloned.1.call-start = ((), (), s32[]{:S(2)}) async-start(), calls=%async_computation.21 | async-start | bytes 524288 | tf_op jit(solution)/shard_map/psum | solution.py:164
  933.6 3.7 collective-permute-start.3
  945.8 92.2 %all-gather.36.cloned.1.call-start = ((), (), s32[]{:S(2)}) async-start(), calls=%async_computation.23 | async-start | bytes 1179648 | tf_op jit(solution)/shard_map/all_gather | solution.py:177
  954.4 150.1 %reduce-scatter.29.cloned.1.call-start = ((), (), s32[]{:S(2)}) async-start(), calls=%async_computation.30 | async-start | bytes 1179648
  1009.4 162.1 %reduce-scatter.27.cloned.1.call-start = ((), (), s32[]{:S(2)}) async-start(), calls=%async_computation.29 | async-start | bytes 1179648
  1050.0 158.4 %all-reduce.30.cloned.1.call-start = ((), (), s32[]{:S(2)}) async-start(), calls=%async_computation.32 | async-start | bytes 1048576 | tf_op jit(solution)/shard_map/psum | solution.py:114
  1063.4 112.4 %copy-start.45 = (bf16[128,2048]{1,0:T(8,128)(2,1)S(1)}, bf16[128,2048]{1,0:T(8,128)(2,1)}, u32[]{:S(2)}) copy-start(bf16[128,2048]{1,0:T(8,128)(2,1)} %copy-done.44) | copy-start | bytes 1572868
  1066.6 118.9 %copy-start.57 = (bf16[8,64,128]{2,1,0:T(8,128)(2,1)}, bf16[8,64,128]{2,1,0:T(8,128)(2,1)S(1)}, u32[]{:S(2)}) copy-start(bf16[8,64,128]{2,1,0:T(8,128)(2,1)S(1)} %get-tuple-element.115) | copy-start | bytes 393220
  1066.6 109.3 %copy-start.89 = (f32[1,1,1024]{2,1,0:T(1,128)S(1)}, f32[1,1,1024]{2,1,0:T(1,128)}, u32[]{:S(2)}) copy-start(f32[1,1,1024]{2,1,0:T(1,128)} %copy-done.86) | copy-start | bytes 12292
  1066.6 109.3 %copy-start.131 = (f32[128]{0:T(128)S(1)}, f32[128]{0:T(128)}, u32[]{:S(2)}) copy-start(f32[128]{0:T(128)} %copy-done.129) | copy-start | bytes 1540
  1066.6 109.3 %copy-start.135 = (f32[128]{0:T(128)S(1)}, f32[128]{0:T(128)}, u32[]{:S(2)}) copy-start(f32[128]{0:T(128)} %copy-done.132) | copy-start | bytes 1540
  1066.6 109.3 %copy-start.138 = (f32[128]{0:T(128)S(1)}, f32[128]{0:T(128)}, u32[]{:S(2)}) copy-start(f32[128]{0:T(128)} %copy-done.136) | copy-start | bytes 1540
  1066.6 109.3 %copy-start.142 = (f32[128]{0:T(128)S(1)}, f32[128]{0:T(128)}, u32[]{:S(2)}) copy-start(f32[128]{0:T(128)} %copy-done.139) | copy-start | bytes 1540
  1105.5 84.9 %copy-start.47 = (bf16[128,512]{0,1:T(8,128)(2,1)}, bf16[128,512]{0,1:T(8,128)(2,1)S(1)}, u32[]{:S(2)}) copy-start(bf16[128,512]{0,1:T(8,128)(2,1)S(1)} %copy.111) | copy-start | bytes 393220
  1175.8 331.2 %all-reduce.28.cloned.1.call-start = ((), (), s32[]{:S(2)}) async-start(), calls=%async_computation.31 | async-start | bytes 18874368 | tf_op jit(solution)/shard_map/psum | solution.py:320
  1187.1 800.9 %all-gather.38.cloned.1.call-start = ((), (), s32[]{:S(2)}) async-start(), calls=%async_computation.24 | async-start | bytes 28311552 | tf_op jit(solution)/shard_map/all_gather | solution.py:316
  1198.1 54.1 %copy-start.82 = (bf16[128,1024]{1,0:T(8,128)(2,1)S(1)}, bf16[128,1024]{1,0:T(8,128)(2,1)}, u32[]{:S(2)}) copy-start(bf16[128,1024]{1,0:T(8,128)(2,1)} %copy-done.81) | copy-start | bytes 786436
  1198.1 54.1 %copy-start.105 = (f32[1,1024]{1,0:T(1,128)S(1)}, f32[1,1024]{1,0:T(1,128)}, u32[]{:S(2)}) copy-start(f32[1,1024]{1,0:T(1,128)} %copy-done.103) | copy-start | bytes 12292
  1202.8 52.3 %copy-start.32 = (f32[128,1024]{1,0:T(8,128)S(1)}, f32[128,1024]{1,0:T(8,128)}, u32[]{:S(2)}) copy-start(f32[128,1024]{1,0:T(8,128)} %copy-done.31) | copy-start | bytes 1572868
  1202.8 53.6 %copy-start.49 = (f32[1,128,1024]{2,1,0:T(8,128)S(1)}, f32[1,128,1024]{2,1,0:T(8,128)}, u32[]{:S(2)}) copy-start(f32[1,128,1024]{2,1,0:T(8,128)} %get-tuple-element.69) | copy-start | bytes 1572868
  (136 other events, 1462.9 us)
Sparse Core Ops, SparseCore 0:
  19.9 42.9 all-gather.15
  65.1 38.9 all-gather.13
  109.9 21.9 all-reduce.15
  139.5 23.2 all-reduce.17
  173.0 40.2 all-gather.19
  215.3 38.9 all-gather.17
  261.2 21.9 all-reduce.19
  297.3 28.6 all-reduce.33
  328.6 40.2 all-gather.25
  370.9 38.9 all-gather.23
  412.1 38.9 all-gather.27
  453.1 38.9 all-gather.21
  495.5 62.9 reduce-scatter.20
  562.3 63.1 reduce-scatter.18
  630.0 27.5 all-reduce.31
  660.1 40.2 all-gather.29
  703.1 21.9 all-reduce.21
  727.2 40.2 all-gather.31
  771.4 62.8 reduce-scatter.24
  837.6 63.1 reduce-scatter.22
  906.0 22.3 all-reduce.23
  930.5 40.2 all-gather.33
  973.7 21.9 all-reduce.25
  997.7 40.2 all-gather.35
  1041.4 63.0 reduce-scatter.28
  1108.3 63.1 reduce-scatter.26
  1175.9 27.6 all-reduce.29
  1208.5 298.4 all-reduce.27
  1508.5 479.3 all-gather.37
